TPU v7x, 32 devices: a whole 2x2x4 slice. The times are simulated.
32 devices in a mesh: row: 8 (over z, y), col: 4 (over x, core).
Axes of the slice: x: 2, y: 2, z: 4, core: 2. Of those that a mesh axis runs over, the one named last changes fastest.
Arguments:
- sequence: bfloat16 [128, 1024], P('row'), may hold values from -6 to 6
- pair_state: bfloat16 [128, 128, 128], P('row', 'col'), may hold values from -6 to 6
- residue_mask: int32 [128], replicated, may hold values 0 or 1
- chain_index: int32 [128], replicated, may hold values from 0 to 3, never falling along the last dimension, each value on 1 to 64 neighbouring positions
- attention_in: bfloat16 [1024, 4, 1024], P(None, None, 'col'), may hold values from -0.1875 to 0.1875
- attention_out: bfloat16 [1024, 1024], P('col'), may hold values from -0.1875 to 0.1875
- bias_weight: bfloat16 [128, 32], replicated, may hold values from -40 to 40
- chain_bias: float32 [32], replicated, may hold values from -2 to 2
- outer_in: bfloat16 [1024, 128], replicated, may hold values from -0.1875 to 0.1875
- outer_out: bfloat16 [128, 128], replicated, may hold values from -0.5 to 0.5
- triangle_in: bfloat16 [128, 5, 128], replicated, may hold values from -0.5 to 0.5
- triangle_out: bfloat16 [128, 128], replicated, may hold values from -0.5 to 0.5
- transition_up: bfloat16 [128, 512], replicated, may hold values from -0.5 to 0.5
- transition_down: bfloat16 [512, 128], replicated, may hold values from -0.25 to 0.25
Outputs:
- sequence_out: bfloat16 [128, 1024], P('row')
- pair_out: bfloat16 [128, 128, 128], P('row', 'col')
Inputs may be any that keep to these rules, and one draw needn't show every extreme that they name: chain_index never falls along the residues; each chain holds at most 64 residues.
All inputs are finite; a program needn't handle non-finite values.
Results may differ from a plain program's by a relative error of at most 0.0095.
The roundings to bfloat16 on the way count: a program that leaves them out, or rounds other values in their place, can miss the bound.
Values may be sent and summed in bfloat16 or wider, within the bound.
A program may use at most 64 MiB of HBM per device.

v0:
```python
import math

import jax
import jax.numpy as jnp
from jax import lax
from jax.sharding import PartitionSpec as P


def layer_norm(values):
    center = values - jnp.mean(values, axis=-1, keepdims=True)
    spread = jnp.mean(center * center, axis=-1, keepdims=True)
    return center * lax.rsqrt(spread + 1e-05)


def per_device(
    sequence,
    pair_state,
    residue_mask,
    chain_index,
    attention_in,
    attention_out,
    bias_weight,
    chain_bias,
    outer_in,
    outer_out,
    triangle_in,
    triangle_out,
    transition_up,
    transition_down,
):
    rows_here, cols_here, channels = pair_state.shape
    length_all = residue_mask.shape[0]
    row_index = lax.axis_index("row")
    col_index = lax.axis_index("col")
    row_start = row_index * rows_here
    col_start = col_index * cols_here
    pair_wide = pair_state.astype(jnp.float32)
    normed_pair = layer_norm(pair_wide).astype(jnp.bfloat16)
    bias_tile = jnp.einsum(
        "ijc,ch->hij", normed_pair, bias_weight, preferred_element_type=jnp.float32
    )
    pair_bias = lax.all_to_all(bias_tile, "col", split_axis=0, concat_axis=2, tiled=True)
    heads_here = pair_bias.shape[0]
    normed_seq = layer_norm(sequence.astype(jnp.float32)).astype(jnp.bfloat16)
    projected = jnp.einsum(
        "id,dpe->ipe", normed_seq, attention_in, preferred_element_type=jnp.float32
    )
    query = projected[:, 0].astype(jnp.bfloat16)
    key_rows = projected[:, 1].astype(jnp.bfloat16)
    value_rows = projected[:, 2].astype(jnp.bfloat16)
    gate = jax.nn.sigmoid(projected[:, 3])
    keys_all, values_all = (
        lax.all_gather(key_rows, "row", axis=0, tiled=True),
        lax.all_gather(value_rows, "row", axis=0, tiled=True),
    )
    head_width = query.shape[1] // heads_here
    query_heads = query.reshape(rows_here, heads_here, head_width)
    key_heads = keys_all.reshape(length_all, heads_here, head_width)
    value_heads = values_all.reshape(length_all, heads_here, head_width)
    scale = 1.0 / math.sqrt(head_width)
    scores = (
        jnp.einsum("ihd,jhd->hij", query_heads, key_heads, preferred_element_type=jnp.float32)
        * scale
    )
    chain_rows = lax.dynamic_slice_in_dim(chain_index, row_start, rows_here, 0)
    same_chain = (chain_rows[:, None] == chain_index[None, :]).astype(jnp.float32)
    head_offset = lax.dynamic_slice_in_dim(chain_bias, col_index * heads_here, heads_here, 0)
    scores = scores + pair_bias + head_offset[:, None, None] * same_chain[None]
    positions = jnp.arange(length_all, dtype=jnp.int32)
    query_ids = row_start + jnp.arange(rows_here, dtype=jnp.int32)
    allowed = (residue_mask[None, :] == 1) | (query_ids[:, None] == positions[None, :])
    allowed = allowed[None]
    highest = jnp.max(jnp.where(allowed, scores, -jnp.inf), axis=-1, keepdims=True)
    raised = jnp.where(allowed, jnp.exp(scores - highest), 0.0)
    weights = (raised / jnp.sum(raised, axis=-1, keepdims=True)).astype(jnp.bfloat16)
    gathered = jnp.einsum(
        "hij,jhd->ihd", weights, value_heads, preferred_element_type=jnp.float32
    ).reshape(rows_here, -1)
    mixed = (gate * gathered).astype(jnp.bfloat16)
    head_terms = jnp.dot(mixed, attention_out, preferred_element_type=jnp.float32)
    update = lax.psum(head_terms, "col")
    sequence_out = (sequence.astype(jnp.float32) + update).astype(jnp.bfloat16)
    normed_out = layer_norm(sequence_out.astype(jnp.float32)).astype(jnp.bfloat16)
    outer_rows = jnp.dot(normed_out, outer_in, preferred_element_type=jnp.float32).astype(
        jnp.bfloat16
    )
    half_width = outer_rows.shape[1] // 2
    right_all = lax.all_gather(outer_rows[:, half_width:], "row", axis=0, tiled=True)
    right_side = lax.dynamic_slice_in_dim(right_all, col_start, cols_here, 0).astype(jnp.float32)
    left_side = outer_rows[:, :half_width].astype(jnp.float32)
    outer_feat = jnp.concatenate(
        [
            left_side[:, None, :] * right_side[None, :, :],
            left_side[:, None, :] - right_side[None, :, :],
        ],
        axis=-1,
    ).astype(jnp.bfloat16)
    pair_mid = pair_wide + jnp.dot(
        outer_feat.reshape(-1, 2 * half_width), outer_out, preferred_element_type=jnp.float32
    ).reshape(rows_here, cols_here, channels)
    normed_mid = layer_norm(pair_mid).astype(jnp.bfloat16)
    tri = jnp.dot(
        normed_mid.reshape(-1, channels),
        triangle_in.reshape(channels, -1),
        preferred_element_type=jnp.float32,
    ).reshape(rows_here, cols_here, 5, channels)
    live = residue_mask.astype(jnp.float32)
    row_live = lax.dynamic_slice_in_dim(live, row_start, rows_here, 0)
    col_live = lax.dynamic_slice_in_dim(live, col_start, cols_here, 0)
    pair_live = (row_live[:, None] * col_live[None, :])[:, :, None]
    left_op = (jax.nn.sigmoid(tri[:, :, 0]) * tri[:, :, 1] * pair_live).astype(jnp.bfloat16)
    right_op = (jax.nn.sigmoid(tri[:, :, 2]) * tri[:, :, 3] * pair_live).astype(jnp.bfloat16)
    out_gate = jax.nn.sigmoid(tri[:, :, 4])
    column_all = lax.all_gather(right_op, "row", axis=0, tiled=True)
    crossed = lax.psum_scatter(
        jnp.einsum("jkc,ikc->jic", column_all, left_op, preferred_element_type=jnp.float32),
        "col",
        scatter_dimension=0,
        tiled=True,
    )
    product = jnp.transpose(crossed, (1, 0, 2))
    normed_product = layer_norm(product).astype(jnp.bfloat16)
    projected_product = jnp.dot(
        normed_product.reshape(-1, channels), triangle_out, preferred_element_type=jnp.float32
    ).reshape(rows_here, cols_here, channels)
    pair_late = pair_mid + out_gate * projected_product
    normed_late = layer_norm(pair_late).astype(jnp.bfloat16)
    hidden = jax.nn.relu(
        jnp.dot(
            normed_late.reshape(-1, channels), transition_up, preferred_element_type=jnp.float32
        )
    ).astype(jnp.bfloat16)
    lowered = jnp.dot(hidden, transition_down, preferred_element_type=jnp.float32).reshape(
        rows_here, cols_here, channels
    )
    pair_out = (pair_late + lowered).astype(jnp.bfloat16)
    return (sequence_out, pair_out)


def solution(mesh):
    return jax.shard_map(
        per_device,
        mesh=mesh,
        in_specs=(
            P("row", None),
            P("row", "col", None),
            P(),
            P(),
            P(None, None, "col"),
            P("col", None),
            P(),
            P(),
            P(),
            P(),
            P(),
            P(),
            P(),
            P(),
        ),
        out_specs=(P("row", None), P("row", "col", None)),
        check_vma=False,
    )
```

profile of v0, /device:TPU:24, one launch (start us, length us, event | category | flops | bytes accessed | tf_op | source)
XLA Modules:
  0.0 255.9 jit_solution(43655018280628967)
XLA Ops:
  7.2 1.2 convert_reduce_fusion
  8.4 1.2 fusion.14
  9.6 1.2 convolution_bitcast_fusion.1
  11.0 0.8 reshape.259
  11.8 3.3 %all-to-all-start = ((f32[4,1,4096]{2,1,0:T(1,128)}), f32[4,1,4096]{2,1,0:T(1,128)S(1)}, u32[]{:S(2)}, u32[]{:S(2)}) async-start(f32[4,1,4096]{2,1,0:T(1,128)} %reshape.259), calls=%async_computation | async-start | bytes 131072 | tf_op jit(solution)/shard_map/all_to_all | solution.py:42
  18.4 0.9 convert_reduce_fusion.1
  19.3 0.9 fusion.50
  21.0 1.9 fusion.92
  23.6 27.8 %all-gather.1 = bf16[128,1,256]{2,0,1:T(8,128)(2,1)S(1)} all-gather(bf16[16,1,256]{2,0,1:T(8,128)(2,1)S(1)} %get-tuple-element.7), channel_id=3, replica_groups=mesh['row'=8,'col'=4] {'row'}, dimensions={0}, use_global_device_ids=true | all-gather | bytes 73728 | tf_op jit(solution)/shard_map/all_gather | solution.py:53
  51.6 30.5 %all-gather = bf16[128,1,256]{2,0,1:T(8,128)(2,1)S(1)} all-gather(bf16[16,1,256]{2,0,1:T(8,128)(2,1)S(1)} %get-tuple-element.8), channel_id=2, replica_groups=mesh['row'=8,'col'=4] {'row'}, dimensions={0}, use_global_device_ids=true | all-gather | bytes 73728 | tf_op jit(solution)/shard_map/all_gather | solution.py:54
  84.7 0.9 fusion.10
  85.9 1.1 convolution_bitcast_fusion.2
  87.1 1.5 fusion.74
  89.5 0.8 copy.95
  90.3 34.2 %all-reduce.2.cloned.1.call-done = f32[16,1024]{1,0:T(8,128)} async-done(((f32[16,1024]{1,0:T(8,128)}), f32[16,1024]{1,0:T(8,128)}) %all-reduce.2.cloned.1.call-update) | async-done | bytes 65552 | tf_op jit(solution)/shard_map/psum | solution.py:81
  124.5 1.0 convert_reduce_fusion.2
  125.9 27.9 %all_gather.14 = bf16[128,64]{1,0:T(8,128)(2,1)S(1)} all-gather(bf16[16,64]{1,0:T(8,128)(2,1)S(1)} %get-tuple-element.12), channel_id=1, replica_groups=mesh['row'=8,'col'=4] {'row'}, dimensions={0}, use_global_device_ids=true | all-gather | bytes 18432 | tf_op jit(solution)/shard_map/all_gather | solution.py:88
  153.9 1.1 fusion.94
  155.7 1.3 fusion.32
  157.1 0.8 fusion.18
  158.0 1.2 copy.101
  159.2 40.6 %all-gather.4.cloned.1.call-done = bf16[128,32,128]{2,1,0:T(8,128)(2,1)} async-done(((bf16[16,32,128]{2,1,0:T(8,128)(2,1)}), bf16[128,32,128]{2,1,0:T(8,128)(2,1)}) %all-gather.4.cloned.1.call-update) | async-done | bytes 1048592 | tf_op jit(solution)/shard_map/all_gather | solution.py:114
  199.8 7.3 %copy.102 = bf16[128,32,128]{1,0,2:T(8,128)(2,1)} copy(bf16[128,32,128]{2,1,0:T(8,128)(2,1)} %all-gather.4.cloned.1.call-done) | data formatting | bytes 2097152 | tf_op jit(solution)/shard_map/all_gather | solution.py:114
  207.0 5.6 %convolution_bitcast_fusion = f32[128,16,128]{0,1,2:T(8,128)} fusion(bf16[16,32,128]{1,0,2:T(8,128)(2,1)} %copy.101, bf16[128,32,128]{1,0,2:T(8,128)(2,1)} %copy.102), kind=kOutput, calls=%fused_computation.4 | convolution fusion | flops 16777216 | bytes 2228224 | tf_op jit(solution)/shard_map/jkc,ikc->jic/dot_general | solution.py:116
  212.6 2.8 %copy.103 = f32[128,16,128]{2,1,0:T(8,128)} copy(f32[128,16,128]{0,1,2:T(8,128)} %convolution_bitcast_fusion) | data formatting | bytes 2097152 | tf_op jit(solution)/shard_map/jkc,ikc->jic/transpose | solution.py:116
  215.4 25.0 %reduce-scatter.2.cloned.1.call-done = f32[32,16,128]{2,1,0:T(8,128)} async-done(((f32[128,16,128]{2,1,0:T(8,128)}), f32[32,16,128]{2,1,0:T(8,128)}) %reduce-scatter.2.cloned.1.call-update) | async-done | bytes 262160 | tf_op jit(solution)/shard_map/reduce_scatter | solution.py:115
  240.4 1.1 bitcast_reduce_fusion
  241.6 1.2 multiply_reduce_fusion.1
  243.0 1.2 multiply_convert_fusion.1
  244.2 1.3 fusion.95
  246.4 1.3 fusion.4
  247.7 1.6 add_convert_fusion
  (76 shorter events, 11.3 us)
Async XLA Ops:
  7.2 13.8 %copy-start = (bf16[1024,4,256]{2,1,0:T(4,128)(2,1)S(1)}, bf16[1024,4,256]{2,1,0:T(4,128)(2,1)}, u32[]{:S(2)}) copy-start(bf16[1024,4,256]{2,1,0:T(4,128)(2,1)} %param.18) | copy-start | bytes 6291460
  9.6 73.3 %copy-start.10 = (f32[32]{0:T(128)S(1)}, f32[32]{0:T(128)}, u32[]{:S(2)}) copy-start(f32[32]{0:T(128)} %param.21) | copy-start | bytes 388
  11.8 71.2 %all-to-all-start = ((f32[4,1,4096]{2,1,0:T(1,128)}), f32[4,1,4096]{2,1,0:T(1,128)S(1)}, u32[]{:S(2)}, u32[]{:S(2)}) async-start(f32[4,1,4096]{2,1,0:T(1,128)} %reshape.259), calls=%async_computation | async-start | bytes 131072 | tf_op jit(solution)/shard_map/all_to_all | solution.py:42
  15.1 109.4 %all-reduce.2.cloned.1.call-start = ((), (), s32[]{:S(2)}) async-start(), calls=%async_computation.2 | async-start | bytes 131072 | tf_op jit(solution)/shard_map/psum | solution.py:81
  21.0 66.2 %copy-start.5 = (bf16[256,1024]{1,0:T(8,128)(2,1)S(1)}, bf16[256,1024]{1,0:T(8,128)(2,1)}, u32[]{:S(2)}) copy-start(bf16[256,1024]{1,0:T(8,128)(2,1)} %param.19) | copy-start | bytes 1572868
  22.9 66.6 %copy-start.6 = (bf16[128,5,128]{2,0,1:T(8,128)(2,1)S(1)}, bf16[128,5,128]{2,0,1:T(8,128)(2,1)}, u32[]{:S(2)}) copy-start(bf16[128,5,128]{2,0,1:T(8,128)(2,1)} %param.24) | copy-start | bytes 491524
  22.9 101.6 %copy-start.4 = (bf16[16,1024]{1,0:T(8,128)(2,1)S(1)}, bf16[16,1024]{1,0:T(8,128)(2,1)}, u32[]{:S(2)}) copy-start(bf16[16,1024]{1,0:T(8,128)(2,1)} %param.14) | copy-start | bytes 98308
  82.8 71.1 %copy-start.3 = (bf16[16,32,128]{2,1,0:T(8,128)(2,1)S(1)}, bf16[16,32,128]{2,1,0:T(8,128)(2,1)}, u32[]{:S(2)}) copy-start(bf16[16,32,128]{2,1,0:T(8,128)(2,1)} %param.15) | copy-start | bytes 393220
  84.7 40.9 %copy-start.8 = (bf16[1024,128]{1,0:T(8,128)(2,1)S(1)}, bf16[1024,128]{1,0:T(8,128)(2,1)}, u32[]{:S(2)}) copy-start(bf16[1024,128]{1,0:T(8,128)(2,1)} %param.22) | copy-start | bytes 786436
  88.7 111.1 %all-gather.4.cloned.1.call-start = ((), (), s32[]{:S(2)}) async-start(), calls=%async_computation.3 | async-start | bytes 1179648 | tf_op jit(solution)/shard_map/all_gather | solution.py:114
  125.4 29.9 %copy-start.7 = (bf16[16,1024]{1,0:T(8,128)(2,1)}, bf16[16,1024]{1,0:T(8,128)(2,1)S(1)}, u32[]{:S(2)}) copy-start(bf16[16,1024]{1,0:T(8,128)(2,1)S(1)} %get-tuple-element.3) | copy-start | bytes 98308
  155.0 0.7 copy-start.2
  157.9 82.5 %reduce-scatter.2.cloned.1.call-start = ((), (), s32[]{:S(2)}) async-start(), calls=%async_computation.4 | async-start | bytes 1310720 | tf_op jit(solution)/shard_map/reduce_scatter | solution.py:115
  244.1 2.2 copy-start.9
  245.5 0.7 copy-start.1
Sparse Core Ops, SparseCore 0:
  88.8 35.6 all-reduce.1
  158.0 41.6 all-gather.3
  215.5 24.8 reduce-scatter.1
where the time goes:
time: 259 us; the launch traced here: 256 us
  waiting for transfers between devices  99.8 us (39%)
  blocking collectives  86.3 us (33%)
  local copies, waits for them, and re-layouts  18.8 us (7%)
  matrix products  17.5 us (7%)
  other arithmetic  16 us (6%)
  between operations  14.1 us (5%)
  starting transfers between devices  3.41 us (1%)
    all_gather x1, waiting for transfers between devices, per_device(): column_all = lax.all_gather(right_op, 'row', axis=0, tiled=True)  40.6 us
    psum x1, waiting for transfers between devices, per_device(): update = lax.psum(head_terms, 'col')  34.2 us
    all_gather x1, blocking collectives, per_device(): lax.all_gather(value_rows, 'row', axis=0, tiled=True)  30.5 us
    all_gather x1, blocking collectives, per_device(): lax.all_gather(outer_rows[:, half_width:], 'row', axis=0, tiled=True)  27.9 us
    all_gather x1, blocking collectives, per_device(): lax.all_gather(key_rows, 'row', axis=0, tiled=True)  27.8 us
    reduce_scatter x1, waiting for transfers between devices, per_device(): lax.psum_scatter(jnp.einsum('jkc,ikc->jic', column_all, left_op, preferre...  25 us
    all_gather x1, local copies, waits for them, and re-layouts, per_device(): column_all = lax.all_gather(right_op, 'row', axis=0, tiled=True)  7.25 us
    dot_general x1, matrix products, per_device(): jnp.einsum('jkc,ikc->jic', column_all, left_op, preferred_element_type=jn...  5.6 us
  transfers between devices with their start and end apart: 4, of which 3 were waited for; matrix products, arithmetic and copies ran while one was open for 5% of the time, Pallas kernels for 0%

commit v1 on v0

v1 whole, which is shorter than its diff:
```python
import functools
import math

import jax
import jax.numpy as jnp
from jax import lax
from jax.experimental import pallas as pl
from jax.experimental.pallas import tpu as pltpu
from jax.sharding import PartitionSpec as P

F32 = jnp.float32
BF16 = jnp.bfloat16
MESH = pl.DeviceIdType.MESH


def layer_norm(values):
    center = values - jnp.mean(values, axis=-1, keepdims=True)
    spread = jnp.mean(center * center, axis=-1, keepdims=True)
    return center * lax.rsqrt(spread + 1e-05)


def nt_dot(a, b):
    return lax.dot_general(a, b, (((1,), (1,)), ((), ())), preferred_element_type=F32)


def kernel(
    nr,
    nc,
    head_width,
    seq_ref,
    pair_ref,
    mask_ref,
    chain_ref,
    proj_ref,
    attn_out_ref,
    bias_w_ref,
    chain_bias_ref,
    outer_in_ref,
    outer_out_ref,
    tri_in_ref,
    tri_out_ref,
    up_ref,
    down_ref,
    seq_out_ref,
    pair_out_ref,
    bias_send,
    bias_recv,
    kv_all,
    base_scores,
    upd,
    outer_all,
    mid_ref,
    norm_ref,
    left_ref,
    right_ref,
    gate_ref,
    right_all,
    prod_ref,
    prod_recv,
    row_send,
    row_recv,
    col_send,
    col_recv,
):
    me_r = lax.axis_index("row")
    me_c = lax.axis_index("col")
    rows, width = seq_ref.shape
    pairs, chan = pair_ref.shape
    cols = pairs // rows
    length = mask_ref.shape[1]
    feats = attn_out_ref.shape[0]
    heads = feats // head_width
    heads_all = chain_bias_ref.shape[1]
    per_col = cols // rows
    row_start = me_r * rows
    col_start = me_c * cols

    def row_peer(d):
        return lax.rem(me_r + d, nr)

    def col_peer(d):
        return lax.rem(me_c + d, nc)

    def row_copy(phase, d, src, dst):
        return pltpu.make_async_remote_copy(
            src_ref=src,
            dst_ref=dst,
            send_sem=row_send.at[phase, d],
            recv_sem=row_recv.at[phase, d],
            device_id=(row_peer(d), me_c),
            device_id_type=MESH,
        )

    def col_copy(phase, d, src, dst):
        return pltpu.make_async_remote_copy(
            src_ref=src,
            dst_ref=dst,
            send_sem=col_send.at[phase, d],
            recv_sem=col_recv.at[phase, d],
            device_id=(me_r, col_peer(d)),
            device_id_type=MESH,
        )

    barrier = pltpu.get_barrier_semaphore()
    for d in range(1, nr):
        pl.semaphore_signal(barrier, inc=1, device_id=(row_peer(d), me_c), device_id_type=MESH)
    for d in range(1, nc):
        pl.semaphore_signal(barrier, inc=1, device_id=(me_r, col_peer(d)), device_id_type=MESH)

    my_rows = pl.ds(pl.multiple_of(row_start, rows), rows)
    kv_all[my_rows, :] = proj_ref[:, feats : 3 * feats].astype(BF16)
    pl.semaphore_wait(barrier, nr + nc - 2)
    kv_copies = []
    for d in range(1, nr):
        kv_copies.append(row_copy(0, d, kv_all.at[my_rows, :], kv_all.at[my_rows, :]))
        kv_copies[-1].start()
    normed_pair = layer_norm(pair_ref[...].astype(F32)).astype(BF16)
    bias_t = bias_w_ref[...].astype(F32).T.astype(BF16)
    tile = nt_dot(bias_t, normed_pair)
    for c in range(nc):
        bias_send[c] = tile[c * heads : (c + 1) * heads, :]
    bias_copies = []
    for d in range(1, nc):
        bias_copies.append(col_copy(0, d, bias_send.at[col_peer(d)], bias_recv.at[me_c]))
        bias_copies[-1].start()
    bias_recv[me_c] = bias_send[me_c]

    lane_l = lax.broadcasted_iota(jnp.int32, (rows, length), 1)
    sub_l = lax.broadcasted_iota(jnp.int32, (rows, length), 0)
    mine = lane_l == sub_l + row_start
    chain_row = chain_ref[...]
    mask_row = mask_ref[...]
    chain_col = jnp.sum(
        jnp.where(mine, chain_row.astype(F32), 0.0), axis=-1, keepdims=True
    )
    allowed = jnp.logical_or(mask_row == 1, mine)
    same = (chain_col == chain_row.astype(F32)).astype(F32)
    blocked = jnp.where(allowed, 0.0, -jnp.inf)
    hl = lax.broadcasted_iota(jnp.int32, (heads, heads_all), 1)
    hs = lax.broadcasted_iota(jnp.int32, (heads, heads_all), 0)
    offset = jnp.sum(
        jnp.where(hl == hs + me_c * heads, chain_bias_ref[...], 0.0), axis=-1, keepdims=True
    )
    head_lane = lax.broadcasted_iota(jnp.int32, (heads, feats), 1) // head_width
    own_head = head_lane == lax.broadcasted_iota(jnp.int32, (heads, feats), 0)
    query = proj_ref[:, :feats].astype(BF16).astype(F32)
    gate = jax.nn.sigmoid(proj_ref[:, 3 * feats :])
    query_big = jnp.concatenate(
        [jnp.where(own_head, query[i : i + 1, :], 0.0) for i in range(rows)], axis=0
    ).astype(BF16)

    for copy in bias_copies:
        copy.wait()
    lanes = 128
    per_vreg = lanes // cols
    lane_v = lax.broadcasted_iota(jnp.int32, (heads, lanes), 1) // cols
    for i in range(rows):
        g, s = divmod(i, per_vreg)
        for t in range(length // lanes):
            got = None
            for q in range(per_vreg):
                piece = bias_recv[t * per_vreg + q, :, g * lanes : (g + 1) * lanes]
                shift = (q - s) % per_vreg * cols
                if shift:
                    piece = pltpu.roll(piece, shift, 1)
                got = piece if got is None else jnp.where(lane_v == q, piece, got)
            window = slice(t * lanes, (t + 1) * lanes)
            base_scores[i * heads : (i + 1) * heads, window] = (
                got + offset * same[i : i + 1, window] + blocked[i : i + 1, window]
            )
    for copy in kv_copies:
        copy.wait()
    scores = nt_dot(query_big, kv_all[:, :feats]) * (1.0 / math.sqrt(head_width))
    scores = scores + base_scores[...]
    highest = jnp.max(scores, axis=-1, keepdims=True)
    raised = jnp.exp(scores - highest)
    weights = (raised / jnp.sum(raised, axis=-1, keepdims=True)).astype(BF16)
    spread_out = jnp.dot(weights, kv_all[:, feats:], preferred_element_type=F32)
    gathered = jnp.concatenate(
        [
            jnp.sum(
                jnp.where(own_head, spread_out[i * heads : (i + 1) * heads, :], 0.0),
                axis=0,
                keepdims=True,
            )
            for i in range(rows)
        ],
        axis=0,
    )
    mixed = (gate * gathered).astype(BF16)
    upd[me_c] = jnp.dot(mixed, attn_out_ref[...], preferred_element_type=F32).astype(BF16)
    upd_copies = []
    for d in range(1, nc):
        upd_copies.append(col_copy(1, d, upd.at[me_c], upd.at[me_c]))
        upd_copies[-1].start()
    for copy in upd_copies:
        copy.wait()
    update = upd[0].astype(F32)
    for c in range(1, nc):
        update = update + upd[c].astype(F32)
    sequence_out = (seq_ref[...].astype(F32) + update).astype(BF16)
    seq_out_ref[...] = sequence_out
    normed_out = layer_norm(sequence_out.astype(F32)).astype(BF16)
    outer_rows = jnp.dot(normed_out, outer_in_ref[...], preferred_element_type=F32).astype(BF16)
    outer_all[my_rows, :] = outer_rows
    outer_copies = []
    for d in range(1, nr):
        outer_copies.append(row_copy(1, d, outer_all.at[my_rows, :], outer_all.at[my_rows, :]))
        outer_copies[-1].start()
    half = outer_rows.shape[1] // 2
    left_rows = outer_rows.astype(F32)
    low_r = lax.broadcasted_iota(jnp.int32, (rows, 2 * half), 1) < half
    left_rows = jnp.where(low_r, left_rows, pltpu.roll(left_rows, half, 1))
    live_row = mask_row.astype(F32)
    live_i = jnp.sum(jnp.where(mine, live_row, 0.0), axis=-1, keepdims=True)
    lane_c = lax.broadcasted_iota(jnp.int32, (cols, length), 1)
    sub_c = lax.broadcasted_iota(jnp.int32, (cols, length), 0)
    live_k = jnp.sum(
        jnp.where(lane_c == sub_c + col_start, live_row, 0.0), axis=-1, keepdims=True
    )
    for copy in outer_copies:
        copy.wait()
    right_rows = outer_all[pl.ds(pl.multiple_of(col_start, cols), cols), :].astype(F32)
    low_c = lax.broadcasted_iota(jnp.int32, (cols, 2 * half), 1) < half
    right_rows = jnp.where(low_c, pltpu.roll(right_rows, half, 1), right_rows)
    for i in range(rows):
        left_i = left_rows[i : i + 1, :]
        feat = jnp.where(low_c, left_i * right_rows, left_i - right_rows).astype(BF16)
        norm_ref[i * cols : (i + 1) * cols, :] = feat
    mid = pair_ref[...].astype(F32) + jnp.dot(
        norm_ref[...], outer_out_ref[...], preferred_element_type=F32
    )
    mid_ref[...] = mid
    normed_mid = layer_norm(mid).astype(BF16)
    norm_ref[...] = normed_mid

    tri_r = jnp.dot(
        normed_mid, tri_in_ref[:, 2 * chan : 4 * chan], preferred_element_type=F32
    )
    right_ref[...] = jax.nn.sigmoid(tri_r[:, :chan]) * tri_r[:, chan:]
    for k in range(cols):
        block = right_ref[pl.ds(k, rows, stride=cols), :]
        right_all[me_r, k] = (block * (live_i * live_k[k : k + 1, :])).astype(BF16)
    right_copies = []
    for d in range(1, nr):
        right_copies.append(row_copy(2, d, right_all.at[me_r], right_all.at[me_r]))
        right_copies[-1].start()
    tri_l = jnp.dot(norm_ref[...], tri_in_ref[:, : 2 * chan], preferred_element_type=F32)
    left_raw = jax.nn.sigmoid(tri_l[:, :chan]) * tri_l[:, chan:]
    for i in range(rows):
        window = slice(i * cols, (i + 1) * cols)
        left_ref[window, :] = (
            (left_raw[window, :] * (live_i[i : i + 1, :] * live_k)).astype(BF16).astype(F32)
        )
    gate_ref[...] = jax.nn.sigmoid(
        jnp.dot(norm_ref[...], tri_in_ref[:, 4 * chan :], preferred_element_type=F32)
    )

    def one_block(slot):
        def step(k, sums):
            right_k = right_all[slot, k].astype(F32)
            return tuple(
                sums[i] + left_ref[pl.ds(i * cols + k, 1), :] * right_k for i in range(rows)
            )

        sums = lax.fori_loop(
            0, cols, step, tuple(jnp.zeros((rows, chan), F32) for _ in range(rows))
        )
        for i in range(rows):
            prod_ref[slot, i] = sums[i].astype(BF16)

    one_block(me_r)
    for d in range(1, nr):
        right_copies[d - 1].wait()
        one_block(lax.rem(me_r + nr - d, nr))
    prod_copies = []
    for d in range(1, nc):
        theirs = pl.ds(col_peer(d) * per_col, per_col)
        prod_copies.append(col_copy(2, d, prod_ref.at[theirs], prod_recv.at[me_c]))
        prod_copies[-1].start()
    prod_recv[me_c] = prod_ref[pl.ds(me_c * per_col, per_col)]
    for copy in prod_copies:
        copy.wait()
    for i in range(rows):
        for b in range(per_col):
            total = prod_recv[0, b, i].astype(F32)
            for c in range(1, nc):
                total = total + prod_recv[c, b, i].astype(F32)
            start = i * cols + b * rows
            norm_ref[start : start + rows, :] = layer_norm(total).astype(BF16)
    late = mid_ref[...] + gate_ref[...] * jnp.dot(
        norm_ref[...], tri_out_ref[...], preferred_element_type=F32
    )
    normed_late = layer_norm(late).astype(BF16)
    hidden = jnp.maximum(
        jnp.dot(normed_late, up_ref[...], preferred_element_type=F32), 0.0
    ).astype(BF16)
    lowered = jnp.dot(hidden, down_ref[...], preferred_element_type=F32)
    pair_out_ref[...] = (late + lowered).astype(BF16)


def per_device(
    nr,
    nc,
    sequence,
    pair_state,
    residue_mask,
    chain_index,
    attention_in,
    attention_out,
    bias_weight,
    chain_bias,
    outer_in,
    outer_out,
    triangle_in,
    triangle_out,
    transition_up,
    transition_down,
):
    rows, cols, chan = pair_state.shape
    width = sequence.shape[1]
    length = residue_mask.shape[0]
    feats = attention_out.shape[0]
    heads_all = chain_bias.shape[0]
    heads = heads_all // nc
    head_width = feats // heads
    normed_seq = layer_norm(sequence.astype(F32)).astype(BF16)
    projected = jnp.einsum(
        "id,dpe->ipe", normed_seq, attention_in, preferred_element_type=F32
    ).reshape(rows, 4 * feats)
    pairs = rows * cols
    per_col = cols // rows
    vmem = pl.BlockSpec(memory_space=pltpu.VMEM)
    sequence_out, pair_out = pl.pallas_call(
        functools.partial(kernel, nr, nc, head_width),
        out_shape=(
            jax.ShapeDtypeStruct((rows, width), BF16),
            jax.ShapeDtypeStruct((pairs, chan), BF16),
        ),
        in_specs=[vmem] * 14,
        out_specs=(vmem, vmem),
        scratch_shapes=[
            pltpu.VMEM((nc, heads, pairs), F32),
            pltpu.VMEM((nc, heads, pairs), F32),
            pltpu.VMEM((length, 2 * feats), BF16),
            pltpu.VMEM((rows * heads, length), F32),
            pltpu.VMEM((nc, rows, width), BF16),
            pltpu.VMEM((length, outer_in.shape[1]), BF16),
            pltpu.VMEM((pairs, chan), F32),
            pltpu.VMEM((pairs, chan), BF16),
            pltpu.VMEM((pairs, chan), F32),
            pltpu.VMEM((pairs, chan), F32),
            pltpu.VMEM((pairs, chan), F32),
            pltpu.VMEM((nr, cols, rows, chan), BF16),
            pltpu.VMEM((nr, rows, rows, chan), BF16),
            pltpu.VMEM((nc, per_col, rows, rows, chan), BF16),
            pltpu.SemaphoreType.DMA((3, nr)),
            pltpu.SemaphoreType.DMA((3, nr)),
            pltpu.SemaphoreType.DMA((3, nc)),
            pltpu.SemaphoreType.DMA((3, nc)),
        ],
        compiler_params=pltpu.CompilerParams(
            collective_id=0, has_side_effects=True, vmem_limit_bytes=48 * 1024 * 1024
        ),
    )(
        sequence,
        pair_state.reshape(pairs, chan),
        residue_mask.reshape(1, length),
        chain_index.reshape(1, length),
        projected,
        attention_out,
        bias_weight,
        chain_bias.reshape(1, heads_all),
        outer_in,
        outer_out,
        triangle_in.reshape(chan, 5 * chan),
        triangle_out,
        transition_up,
        transition_down,
    )
    return sequence_out, pair_out.reshape(rows, cols, chan)


def solution(mesh):
    return jax.shard_map(
        functools.partial(per_device, mesh.shape["row"], mesh.shape["col"]),
        mesh=mesh,
        in_specs=(
            P("row", None),
            P("row", "col", None),
            P(),
            P(),
            P(None, None, "col"),
            P("col", None),
            P(),
            P(),
            P(),
            P(),
            P(),
            P(),
            P(),
            P(),
        ),
        out_specs=(P("row", None), P("row", "col", None)),
        check_vma=False,
    )
```

time: 259 us -> 62.4 us (0.24)
  the two profiles are of different devices: /device:TPU:24 before, /device:TPU:31 now
where the time goes in v1:
time: 62.4 us; the launch traced here: 62 us
  Pallas kernels  51.1 us (82%)
  local copies, waits for them, and re-layouts  6.89 us (11%)
  other arithmetic  2 us (3%)
  matrix products  1.18 us (2%)
  between operations  0.82 us (1%)
    pallas_call x1, Pallas kernels, per_device(): pl.pallas_call(functools.partial(kernel, nr, nc, head_width), out_shape=(...  51.1 us
    unnamed x32, local copies, waits for them, and re-layouts  5.82 us

profile of v1, /device:TPU:31, one launch (start us, length us, event | category | flops | bytes accessed | tf_op | source)
XLA Modules:
  0.0 62.0 jit_solution(106216354868864811)
XLA Ops:
  0.6 0.0 copy-start
  0.6 0.0 copy-start.1
  0.7 0.0 copy-start.6
  0.7 0.0 copy-start.5
  0.7 0.0 copy-start.13
  0.7 0.0 copy-start.3
  0.7 0.0 copy-start.12
  0.7 0.0 copy-start.2
  0.7 0.0 copy-start.11
  0.7 0.0 copy-start.10
  0.7 0.0 copy-start.4
  0.8 1.0 %convert_reduce_fusion = f32[16]{0:T(128)S(1)} fusion(bf16[16,1024]{1,0:T(8,128)(2,1)} %seq_ref.1), kind=kLoop, calls=%fused_computation.4 | loop fusion | flops 32752 | bytes 32832 | tf_op jit(solution)/shard_map/reduce_sum | solution.py:17
  1.8 0.9 %fusion.7 = f32[16]{0:T(128)S(1)} fusion(bf16[16,1024]{1,0:T(8,128)(2,1)} %seq_ref.1, f32[16]{0:T(128)S(1)} %broadcast_multiply_fusion), kind=kLoop, calls=%fused_computation.7 | loop fusion | flops 65520 | bytes 32896 | tf_op jit(solution)/shard_map/reduce_sum | solution.py:18
  2.8 1.4 %copy.23.bias_w_ref = bf16[128,32]{1,0:T(8,128)(2,1)} copy(bf16[128,32]{0,1:T(8,128)(2,1)} %param.20) | data formatting | bytes 16384 | tf_op args[6]
  4.2 1.2 %fusion.2 = f32[4,2,8,256]{3,2,1,0:T(8,128)S(1)} fusion(bf16[1024,4,256]{2,1,0:T(4,128)(2,1)S(1)} %copy-done, bf16[16,1024]{1,0:T(8,128)(2,1)} %seq_ref.1, f32[16]{0:T(128)S(1)} %add_rsqrt_fusion, f32[16]{0:T(128)S(1)} %broadcast_multiply_fusion), kind=kOutput, calls=%fused_computation.2 | convolution fusion | flops 33619968 | bytes 2195584 | tf_op jit(solution)/shard_map/id,dpe->ipe/dot_general | solution.py:328
  5.4 0.8 %copy.22 = bf16[128,5,128]{0,2,1:T(8,128)(2,1)} copy(bf16[128,5,128]{2,0,1:T(8,128)(2,1)S(1)} %copy-done.13) | data formatting | bytes 327680 | tf_op args[10]
  6.2 1.1 %copy.24.tri_in_ref = bf16[128,640]{1,0:T(8,128)(2,1)S(1)} copy(bf16[128,640]{0,1:T(8,128)(2,1)} %bitcast.18) | data formatting | bytes 327680 | tf_op jit(solution)/shard_map/reshape | solution.py:376
  7.2 0.0 copy-done.1
  7.2 0.0 copy-done.6
  7.3 0.0 copy-done.5
  7.3 0.0 copy-done.3
  7.3 0.0 copy-done.12
  7.3 0.0 copy-done.2
  7.3 0.0 copy-done.11
  7.3 0.0 copy-done.10
  7.3 0.0 copy-start.7
  7.3 0.7 %copy-done.7 = bf16[128,32]{1,0:T(8,128)(2,1)S(1)} copy-done((bf16[128,32]{1,0:T(8,128)(2,1)S(1)}, bf16[128,32]{1,0:T(8,128)(2,1)}, u32[]{:S(2)}) %copy-start.7) | copy-done | bytes 8216
  8.1 0.8 %copy-done.8 = bf16[128,128]{1,0:T(8,128)(2,1)S(1)} copy-done((bf16[128,128]{1,0:T(8,128)(2,1)S(1)}, bf16[128,128]{1,0:T(8,128)(2,1)}, u32[]{:S(2)}) %copy-start.8) | copy-done | bytes 32792
  8.9 0.8 %copy-done.9 = bf16[128,128]{1,0:T(8,128)(2,1)S(1)} copy-done((bf16[128,128]{1,0:T(8,128)(2,1)S(1)}, bf16[128,128]{1,0:T(8,128)(2,1)}, u32[]{:S(2)}) %copy-start.9) | copy-done | bytes 32792
  9.6 51.1 %shard_map.149 = (bf16[16,1024]{1,0:T(8,128)(2,1)S(1)}, bf16[512,128]{1,0:T(8,128)(2,1)S(1)}) custom-call(bf16[16,1024]{1,0:T(8,128)(2,1)S(1)} %copy-done.1, bf16[512,128]{1,0:T(8,128)(2,1)S(1)} %bitcast.13, s32[1,128]{1,0:T(1,128)S(1)} %bitcast.15, s32[1,128]{1,0:T(1,128)S(1)} %bitcast.16, f32[16,1024]{1,0:T(8,128)S(1)} %bitcast.12, ...), custom_call_target="tpu_custom_call" | custom-call | tf_op jit(solution)/shard_map/pallas_call | solution.py:334
  60.7 0.6 copy.32
  61.3 0.7 %copy.33 = bf16[16,32,128]{2,1,0:T(8,128)(2,1)} copy(bf16[16,32,128]{2,1,0:T(8,128)(2,1)S(1)} %bitcast.14) | data formatting | bytes 262144
  (8 shorter events, 0.0 us)
Async XLA Ops:
  0.6 3.5 %copy-start = (bf16[1024,4,256]{2,1,0:T(4,128)(2,1)S(1)}, bf16[1024,4,256]{2,1,0:T(4,128)(2,1)}, u32[]{:S(2)}) copy-start(bf16[1024,4,256]{2,1,0:T(4,128)(2,1)} %param.18) | copy-start | bytes 6291460
  0.6 6.6 %copy-start.1 = (bf16[16,1024]{1,0:T(8,128)(2,1)S(1)}, bf16[16,1024]{1,0:T(8,128)(2,1)}, u32[]{:S(2)}) copy-start(bf16[16,1024]{1,0:T(8,128)(2,1)} %seq_ref.1) | copy-start | bytes 98308
  0.7 6.6 %copy-start.6 = (bf16[512,128]{1,0:T(8,128)(2,1)S(1)}, bf16[512,128]{1,0:T(8,128)(2,1)}, u32[]{:S(2)}) copy-start(bf16[512,128]{1,0:T(8,128)(2,1)} %down_ref.1) | copy-start | bytes 393220
  0.7 6.6 %copy-start.5 = (bf16[128,512]{1,0:T(8,128)(2,1)S(1)}, bf16[128,512]{1,0:T(8,128)(2,1)}, u32[]{:S(2)}) copy-start(bf16[128,512]{1,0:T(8,128)(2,1)} %up_ref.1) | copy-start | bytes 393220
  0.7 4.7 %copy-start.13 = (bf16[128,5,128]{2,0,1:T(8,128)(2,1)S(1)}, bf16[128,5,128]{2,0,1:T(8,128)(2,1)}, u32[]{:S(2)}) copy-start(bf16[128,5,128]{2,0,1:T(8,128)(2,1)} %param.24) | copy-start | bytes 491524
  0.7 6.6 %copy-start.3 = (bf16[1024,128]{1,0:T(8,128)(2,1)S(1)}, bf16[1024,128]{1,0:T(8,128)(2,1)}, u32[]{:S(2)}) copy-start(bf16[1024,128]{1,0:T(8,128)(2,1)} %outer_in_ref.1) | copy-start | bytes 786436
  0.7 6.6 %copy-start.12 = (f32[32]{0:T(128)S(1)}, f32[32]{0:T(128)}, u32[]{:S(2)}) copy-start(f32[32]{0:T(128)} %param.21) | copy-start | bytes 388
  0.7 6.6 %copy-start.2 = (bf16[256,1024]{1,0:T(8,128)(2,1)S(1)}, bf16[256,1024]{1,0:T(8,128)(2,1)}, u32[]{:S(2)}) copy-start(bf16[256,1024]{1,0:T(8,128)(2,1)} %attn_out_ref.1) | copy-start | bytes 1572868
  0.7 6.6 %copy-start.11 = (s32[128]{0:T(128)S(1)}, s32[128]{0:T(128)}, u32[]{:S(2)}) copy-start(s32[128]{0:T(128)} %param.17) | copy-start | bytes 1540
  0.7 6.6 %copy-start.10 = (s32[128]{0:T(128)S(1)}, s32[128]{0:T(128)}, u32[]{:S(2)}) copy-start(s32[128]{0:T(128)} %param.16) | copy-start | bytes 1540
  0.7 6.6 %copy-start.4 = (bf16[16,32,128]{2,1,0:T(8,128)(2,1)S(1)}, bf16[16,32,128]{2,1,0:T(8,128)(2,1)}, u32[]{:S(2)}) copy-start(bf16[16,32,128]{2,1,0:T(8,128)(2,1)} %param.15) | copy-start | bytes 393220
  7.3 0.8 %copy-start.7 = (bf16[128,32]{1,0:T(8,128)(2,1)S(1)}, bf16[128,32]{1,0:T(8,128)(2,1)}, u32[]{:S(2)}) copy-start(bf16[128,32]{1,0:T(8,128)(2,1)} %copy.23.bias_w_ref) | copy-start | bytes 24580
  8.1 0.8 %copy-start.8 = (bf16[128,128]{1,0:T(8,128)(2,1)S(1)}, bf16[128,128]{1,0:T(8,128)(2,1)}, u32[]{:S(2)}) copy-start(bf16[128,128]{1,0:T(8,128)(2,1)} %outer_out_ref.1) | copy-start | bytes 98308
  8.8 0.8 %copy-start.9 = (bf16[128,128]{1,0:T(8,128)(2,1)S(1)}, bf16[128,128]{1,0:T(8,128)(2,1)}, u32[]{:S(2)}) copy-start(bf16[128,128]{1,0:T(8,128)(2,1)} %tri_out_ref.1) | copy-start | bytes 98308

commit v2 on v1

--- a/solution.py
+++ b/solution.py
@@ -36,11 +36,11 @@
     bias_w_ref,
     chain_bias_ref,
     outer_in_ref,
-    outer_out_ref,
     tri_in_ref,
-    tri_out_ref,
-    up_ref,
-    down_ref,
+    outer_out_hbm,
+    tri_out_hbm,
+    up_hbm,
+    down_hbm,
     seq_out_ref,
     pair_out_ref,
     bias_send,
@@ -52,15 +52,24 @@
     mid_ref,
     norm_ref,
     left_ref,
+    left_send,
+    left_recv,
     right_ref,
     gate_ref,
     right_all,
     prod_ref,
     prod_recv,
+    outer_out_ref,
+    tri_out_ref,
+    up_ref,
+    down_ref,
     row_send,
     row_recv,
     col_send,
     col_recv,
+    prod_send_sem,
+    prod_recv_sem,
+    load_sem,
 ):
     me_r = lax.axis_index("row")
     me_c = lax.axis_index("col")
@@ -74,6 +83,25 @@
     per_col = cols // rows
     row_start = me_r * rows
     col_start = me_c * cols
+    parity = lax.rem(me_r, 2)
+    partner = me_r + 1 - 2 * parity
+    line = nr // 2
+    me_z = me_r // 2
+    share = per_col // 2
+
+    loads = [
+        pltpu.make_async_copy(src, dst, load_sem.at[n])
+        for n, (src, dst) in enumerate(
+            (
+                (outer_out_hbm, outer_out_ref),
+                (tri_out_hbm, tri_out_ref),
+                (up_hbm, up_ref),
+                (down_hbm, down_ref),
+            )
+        )
+    ]
+    for load in loads:
+        load.start()
 
     def row_peer(d):
         return lax.rem(me_r + d, nr)
@@ -106,19 +134,19 @@
         pl.semaphore_signal(barrier, inc=1, device_id=(row_peer(d), me_c), device_id_type=MESH)
     for d in range(1, nc):
         pl.semaphore_signal(barrier, inc=1, device_id=(me_r, col_peer(d)), device_id_type=MESH)
+        pl.semaphore_signal(barrier, inc=1, device_id=(partner, col_peer(d)), device_id_type=MESH)
 
     my_rows = pl.ds(pl.multiple_of(row_start, rows), rows)
     kv_all[my_rows, :] = proj_ref[:, feats : 3 * feats].astype(BF16)
-    pl.semaphore_wait(barrier, nr + nc - 2)
+    normed_pair = layer_norm(pair_ref[...].astype(F32)).astype(BF16)
+    tile = nt_dot(bias_w_ref[...], normed_pair)
+    for c in range(nc):
+        bias_send[c] = tile[c * heads : (c + 1) * heads, :]
+    pl.semaphore_wait(barrier, nr + 2 * nc - 3)
     kv_copies = []
     for d in range(1, nr):
         kv_copies.append(row_copy(0, d, kv_all.at[my_rows, :], kv_all.at[my_rows, :]))
         kv_copies[-1].start()
-    normed_pair = layer_norm(pair_ref[...].astype(F32)).astype(BF16)
-    bias_t = bias_w_ref[...].astype(F32).T.astype(BF16)
-    tile = nt_dot(bias_t, normed_pair)
-    for c in range(nc):
-        bias_send[c] = tile[c * heads : (c + 1) * heads, :]
     bias_copies = []
     for d in range(1, nc):
         bias_copies.append(col_copy(0, d, bias_send.at[col_peer(d)], bias_recv.at[me_c]))
@@ -218,6 +246,7 @@
     live_k = jnp.sum(
         jnp.where(lane_c == sub_c + col_start, live_row, 0.0), axis=-1, keepdims=True
     )
+    loads[0].wait()
     for copy in outer_copies:
         copy.wait()
     right_rows = outer_all[pl.ds(pl.multiple_of(col_start, cols), cols), :].astype(F32)
@@ -234,53 +263,121 @@
     normed_mid = layer_norm(mid).astype(BF16)
     norm_ref[...] = normed_mid
 
-    tri_r = jnp.dot(
-        normed_mid, tri_in_ref[:, 2 * chan : 4 * chan], preferred_element_type=F32
-    )
-    right_ref[...] = jax.nn.sigmoid(tri_r[:, :chan]) * tri_r[:, chan:]
+    tri_g = jnp.dot(normed_mid, tri_in_ref[2], preferred_element_type=F32)
+    tri_v = jnp.dot(normed_mid, tri_in_ref[3], preferred_element_type=F32)
+    right_ref[...] = jax.nn.sigmoid(tri_g) * tri_v
     for k in range(cols):
         block = right_ref[pl.ds(k, rows, stride=cols), :]
-        right_all[me_r, k] = (block * (live_i * live_k[k : k + 1, :])).astype(BF16)
+        right_all[me_z, k] = (block * (live_i * live_k[k : k + 1, :])).astype(BF16)
     right_copies = []
-    for d in range(1, nr):
-        right_copies.append(row_copy(2, d, right_all.at[me_r], right_all.at[me_r]))
+    for d in range(1, line):
+        right_copies.append(
+            pltpu.make_async_remote_copy(
+                src_ref=right_all.at[me_z],
+                dst_ref=right_all.at[me_z],
+                send_sem=row_send.at[2, d],
+                recv_sem=row_recv.at[2, d],
+                device_id=(lax.rem(me_z + d, line) * 2 + parity, me_c),
+                device_id_type=MESH,
+            )
+        )
         right_copies[-1].start()
-    tri_l = jnp.dot(norm_ref[...], tri_in_ref[:, : 2 * chan], preferred_element_type=F32)
-    left_raw = jax.nn.sigmoid(tri_l[:, :chan]) * tri_l[:, chan:]
+    tri_g = jnp.dot(norm_ref[...], tri_in_ref[0], preferred_element_type=F32)
+    tri_v = jnp.dot(norm_ref[...], tri_in_ref[1], preferred_element_type=F32)
+    left_raw = jax.nn.sigmoid(tri_g) * tri_v
     for i in range(rows):
         window = slice(i * cols, (i + 1) * cols)
-        left_ref[window, :] = (
-            (left_raw[window, :] * (live_i[i : i + 1, :] * live_k)).astype(BF16).astype(F32)
+        rounded = (left_raw[window, :] * (live_i[i : i + 1, :] * live_k)).astype(BF16)
+        left_send[window, :] = rounded
+        left_ref[0, window, :] = rounded.astype(F32)
+    left_copy = pltpu.make_async_remote_copy(
+        src_ref=left_send,
+        dst_ref=left_recv,
+        send_sem=row_send.at[2, 0],
+        recv_sem=row_recv.at[2, 0],
+        device_id=(partner, me_c),
+        device_id_type=MESH,
+    )
+    left_copy.start()
+    gate_ref[...] = jax.nn.sigmoid(
+        jnp.dot(norm_ref[...], tri_in_ref[4], preferred_element_type=F32)
+    )
+
+    def owner_of(slot):
+        block_row = slot * 2 + parity
+        return block_row // per_col, lax.rem(block_row, per_col)
+
+    def prod_copy(which, d, slot):
+        owner, piece = owner_of(slot)
+        apart = lax.rem(me_c + nc - owner, nc)
+        return pltpu.make_async_remote_copy(
+            src_ref=prod_ref.at[which, slot],
+            dst_ref=prod_recv.at[me_c, piece],
+            send_sem=prod_send_sem.at[which, d],
+            recv_sem=prod_recv_sem.at[which, apart * share + piece // 2],
+            device_id=(partner if which else me_r, owner),
+            device_id_type=MESH,
         )
-    gate_ref[...] = jax.nn.sigmoid(
-        jnp.dot(norm_ref[...], tri_in_ref[:, 4 * chan :], preferred_element_type=F32)
-    )
-
-    def one_block(slot):
+
+    def one_block(which, d, slot):
         def step(k, sums):
             right_k = right_all[slot, k].astype(F32)
             return tuple(
-                sums[i] + left_ref[pl.ds(i * cols + k, 1), :] * right_k for i in range(rows)
+                sums[i] + left_ref[which, pl.ds(i * cols + k, 1), :] * right_k
+                for i in range(rows)
             )
 
         sums = lax.fori_loop(
             0, cols, step, tuple(jnp.zeros((rows, chan), F32) for _ in range(rows))
         )
         for i in range(rows):
-            prod_ref[slot, i] = sums[i].astype(BF16)
-
-    one_block(me_r)
-    for d in range(1, nr):
+            prod_ref[which, slot, i] = sums[i].astype(BF16)
+        if which:
+            prod_copy(which, d, slot).start()
+        else:
+            owner, piece = owner_of(slot)
+
+            @pl.when(owner != me_c)
+            def _():
+                prod_copy(which, d, slot).start()
+
+            @pl.when(owner == me_c)
+            def _():
+                prod_recv[me_c, piece] = prod_ref[which, slot]
+
+    slots = [lax.rem(me_z + line - d, line) for d in range(line)]
+    one_block(0, 0, slots[0])
+    left_copy.wait()
+    left_ref[1] = left_recv[...].astype(F32)
+    one_block(1, 0, slots[0])
+    for d in range(1, line):
         right_copies[d - 1].wait()
-        one_block(lax.rem(me_r + nr - d, nr))
-    prod_copies = []
-    for d in range(1, nc):
-        theirs = pl.ds(col_peer(d) * per_col, per_col)
-        prod_copies.append(col_copy(2, d, prod_ref.at[theirs], prod_recv.at[me_c]))
-        prod_copies[-1].start()
-    prod_recv[me_c] = prod_ref[pl.ds(me_c * per_col, per_col)]
-    for copy in prod_copies:
-        copy.wait()
+        one_block(1, d, slots[d])
+        one_block(0, d, slots[d])
+    for e in range(nc):
+        source = lax.rem(me_c + e, nc)
+        for q in range(share):
+            for which in range(2):
+                if e or which:
+                    piece = 2 * q + (1 - parity if which else parity)
+                    pltpu.make_async_remote_copy(
+                        src_ref=prod_ref.at[which, 0],
+                        dst_ref=prod_recv.at[source, piece],
+                        send_sem=prod_send_sem.at[which, 0],
+                        recv_sem=prod_recv_sem.at[which, e * share + q],
+                        device_id=(partner, me_c),
+                        device_id_type=MESH,
+                    ).wait_recv()
+    for d in range(line):
+        prod_copy(1, d, slots[d]).wait_send()
+        owner, _ = owner_of(slots[d])
+
+        @pl.when(owner != me_c)
+        def _():
+            prod_copy(0, d, slots[d]).wait_send()
+
+    for load in loads[1:]:
+        load.wait()
     for i in range(rows):
         for b in range(per_col):
             total = prod_recv[0, b, i].astype(F32)
@@ -337,7 +434,7 @@
             jax.ShapeDtypeStruct((rows, width), BF16),
             jax.ShapeDtypeStruct((pairs, chan), BF16),
         ),
-        in_specs=[vmem] * 14,
+        in_specs=[vmem] * 10 + [pl.BlockSpec(memory_space=pltpu.HBM)] * 4,
         out_specs=(vmem, vmem),
         scratch_shapes=[
             pltpu.VMEM((nc, heads, pairs), F32),
@@ -348,16 +445,25 @@
             pltpu.VMEM((length, outer_in.shape[1]), BF16),
             pltpu.VMEM((pairs, chan), F32),
             pltpu.VMEM((pairs, chan), BF16),
+            pltpu.VMEM((2, pairs, chan), F32),
+            pltpu.VMEM((pairs, chan), BF16),
+            pltpu.VMEM((pairs, chan), BF16),
             pltpu.VMEM((pairs, chan), F32),
             pltpu.VMEM((pairs, chan), F32),
-            pltpu.VMEM((pairs, chan), F32),
-            pltpu.VMEM((nr, cols, rows, chan), BF16),
-            pltpu.VMEM((nr, rows, rows, chan), BF16),
+            pltpu.VMEM((nr // 2, cols, rows, chan), BF16),
+            pltpu.VMEM((2, nr // 2, rows, rows, chan), BF16),
             pltpu.VMEM((nc, per_col, rows, rows, chan), BF16),
+            pltpu.VMEM(outer_out.shape, BF16),
+            pltpu.VMEM(triangle_out.shape, BF16),
+            pltpu.VMEM(transition_up.shape, BF16),
+            pltpu.VMEM(transition_down.shape, BF16),
             pltpu.SemaphoreType.DMA((3, nr)),
             pltpu.SemaphoreType.DMA((3, nr)),
-            pltpu.SemaphoreType.DMA((3, nc)),
-            pltpu.SemaphoreType.DMA((3, nc)),
+            pltpu.SemaphoreType.DMA((2, nc)),
+            pltpu.SemaphoreType.DMA((2, nc)),
+            pltpu.SemaphoreType.DMA((2, nr // 2)),
+            pltpu.SemaphoreType.DMA((2, nc * (per_col // 2))),
+            pltpu.SemaphoreType.DMA((4,)),
         ],
         compiler_params=pltpu.CompilerParams(
             collective_id=0, has_side_effects=True, vmem_limit_bytes=48 * 1024 * 1024
@@ -369,11 +475,11 @@
         chain_index.reshape(1, length),
         projected,
         attention_out,
-        bias_weight,
+        bias_weight.T,
         chain_bias.reshape(1, heads_all),
         outer_in,
+        jnp.transpose(triangle_in, (1, 0, 2)),
         outer_out,
-        triangle_in.reshape(chan, 5 * chan),
         triangle_out,
         transition_up,
         transition_down,

time: 62.4 us -> 44.5 us (0.71)
  the two profiles are of different devices: /device:TPU:31 before, /device:TPU:24 now
where the time goes in v2:
time: 44.5 us; the launch traced here: 44.3 us
  Pallas kernels  38.9 us (87%)
  other arithmetic  1.99 us (4%)
  local copies, waits for them, and re-layouts  1.34 us (3%)
  matrix products  1.18 us (3%)
  between operations  0.86 us (2%)
    pallas_call x1, Pallas kernels, per_device(): pl.pallas_call(functools.partial(kernel, nr, nc, head_width), out_shape=(...  38.9 us
    unnamed x30, local copies, waits for them, and re-layouts  1.34 us
    dot_general x1, matrix products, per_device(): jnp.einsum('id,dpe->ipe', normed_seq, attention_in, preferred_element_typ...  1.18 us
    reduce_sum x1, other arithmetic, layer_norm(): center = values - jnp.mean(values, axis=-1, keepdims=True)  1.03 us
    reduce_sum x1, other arithmetic, layer_norm(): spread = jnp.mean(center * center, axis=-1, keepdims=True)  0.95 us

profile of v2, /device:TPU:24, one launch (start us, length us, event | category | flops | bytes accessed | tf_op | source)
XLA Modules:
  0.0 44.3 jit_solution(8395831487865119719)
XLA Ops:
  0.6 0.0 copy-start
  0.7 0.0 copy-start.1
  0.7 0.0 copy-start.7
  0.7 0.0 copy-start.6
  0.7 0.0 copy-start.9
  0.7 0.0 copy-start.4
  0.7 0.0 copy-start.8
  0.7 0.0 copy-start.3
  0.7 0.0 copy-start.13
  0.7 0.0 copy-start.10
  0.7 0.0 copy-start.2
  0.8 0.0 copy-start.12
  0.8 0.0 copy-start.11
  0.8 0.0 copy-start.5
  0.8 1.0 %convert_reduce_fusion = f32[16]{0:T(128)S(1)} fusion(bf16[16,1024]{1,0:T(8,128)(2,1)} %seq_ref.1), kind=kLoop, calls=%fused_computation.4 | loop fusion | flops 32752 | bytes 32832 | tf_op jit(solution)/shard_map/reduce_sum | solution.py:17
  1.8 0.9 %fusion.7 = f32[16]{0:T(128)S(1)} fusion(bf16[16,1024]{1,0:T(8,128)(2,1)} %seq_ref.1, f32[16]{0:T(128)S(1)} %broadcast_multiply_fusion), kind=kLoop, calls=%fused_computation.7 | loop fusion | flops 65520 | bytes 32896 | tf_op jit(solution)/shard_map/reduce_sum | solution.py:18
  2.8 1.2 %fusion.2 = f32[4,2,8,256]{3,2,1,0:T(8,128)S(1)} fusion(bf16[1024,4,256]{2,1,0:T(4,128)(2,1)S(1)} %copy-done, bf16[16,1024]{1,0:T(8,128)(2,1)} %seq_ref.1, f32[16]{0:T(128)S(1)} %add_rsqrt_fusion, f32[16]{0:T(128)S(1)} %broadcast_multiply_fusion), kind=kOutput, calls=%fused_computation.2 | convolution fusion | flops 33619968 | bytes 2195584 | tf_op jit(solution)/shard_map/id,dpe->ipe/dot_general | solution.py:425
  4.0 0.0 copy-done.7
  4.0 0.0 copy-done.6
  4.0 0.0 copy-done.9
  4.0 0.0 copy-done.4
  4.0 0.0 copy-done.8
  4.0 0.0 copy-done.3
  4.0 0.0 copy-done.13
  4.1 0.0 copy-done.10
  4.1 0.0 copy-done.2
  4.1 0.0 copy-done.12
  4.1 0.0 copy-done.11
  4.1 0.0 copy-done.5
  4.1 38.9 %shard_map.149 = (bf16[16,1024]{1,0:T(8,128)(2,1)S(1)}, bf16[512,128]{1,0:T(8,128)(2,1)S(1)}) custom-call(bf16[16,1024]{1,0:T(8,128)(2,1)S(1)} %copy-done.1, bf16[512,128]{1,0:T(8,128)(2,1)S(1)} %bitcast.15, s32[1,128]{1,0:T(1,128)S(1)} %bitcast.18, s32[1,128]{1,0:T(1,128)S(1)} %bitcast.19, f32[16,1024]{1,0:T(8,128)S(1)} %bitcast.13, ...), custom_call_target="tpu_custom_call" | custom-call | tf_op jit(solution)/shard_map/pallas_call | solution.py:431
  43.0 0.6 %copy.25 = bf16[16,1024]{1,0:T(8,128)(2,1)} copy(bf16[16,1024]{1,0:T(8,128)(2,1)S(1)} %get-tuple-element.8) | data formatting | bytes 65536
  43.6 0.7 %copy.26 = bf16[16,32,128]{2,1,0:T(8,128)(2,1)} copy(bf16[16,32,128]{2,1,0:T(8,128)(2,1)S(1)} %bitcast.16) | data formatting | bytes 262144
  (5 shorter events, 0.0 us)
Async XLA Ops:
  0.6 2.1 %copy-start = (bf16[1024,4,256]{2,1,0:T(4,128)(2,1)S(1)}, bf16[1024,4,256]{2,1,0:T(4,128)(2,1)}, u32[]{:S(2)}) copy-start(bf16[1024,4,256]{2,1,0:T(4,128)(2,1)} %param.18) | copy-start | bytes 6291460
  0.7 3.3 %copy-start.1 = (bf16[16,1024]{1,0:T(8,128)(2,1)S(1)}, bf16[16,1024]{1,0:T(8,128)(2,1)}, u32[]{:S(2)}) copy-start(bf16[16,1024]{1,0:T(8,128)(2,1)} %seq_ref.1) | copy-start | bytes 98308
  0.7 3.3 %copy-start.7 = (bf16[512,128]{1,0:T(8,128)(2,1)S(1)}, bf16[512,128]{1,0:T(8,128)(2,1)}, u32[]{:S(2)}) copy-start(bf16[512,128]{1,0:T(8,128)(2,1)} %down_hbm.1) | copy-start | bytes 393220
  0.7 3.3 %copy-start.6 = (bf16[128,512]{1,0:T(8,128)(2,1)S(1)}, bf16[128,512]{1,0:T(8,128)(2,1)}, u32[]{:S(2)}) copy-start(bf16[128,512]{1,0:T(8,128)(2,1)} %up_hbm.1) | copy-start | bytes 393220
  0.7 3.3 %copy-start.9 = (bf16[128,128]{1,0:T(8,128)(2,1)S(1)}, bf16[128,128]{1,0:T(8,128)(2,1)}, u32[]{:S(2)}) copy-start(bf16[128,128]{1,0:T(8,128)(2,1)} %tri_out_hbm.1) | copy-start | bytes 98308
  0.7 3.3 %copy-start.4 = (bf16[128,5,128]{2,0,1:T(8,128)(2,1)S(1)}, bf16[128,5,128]{2,0,1:T(8,128)(2,1)}, u32[]{:S(2)}) copy-start(bf16[128,5,128]{2,0,1:T(8,128)(2,1)} %param.24) | copy-start | bytes 491524
  0.7 3.3 %copy-start.8 = (bf16[128,128]{1,0:T(8,128)(2,1)S(1)}, bf16[128,128]{1,0:T(8,128)(2,1)}, u32[]{:S(2)}) copy-start(bf16[128,128]{1,0:T(8,128)(2,1)} %outer_out_hbm.1) | copy-start | bytes 98308
  0.7 3.3 %copy-start.3 = (bf16[1024,128]{1,0:T(8,128)(2,1)S(1)}, bf16[1024,128]{1,0:T(8,128)(2,1)}, u32[]{:S(2)}) copy-start(bf16[1024,128]{1,0:T(8,128)(2,1)} %outer_in_ref.1) | copy-start | bytes 786436
  0.7 3.3 %copy-start.13 = (f32[32]{0:T(128)S(1)}, f32[32]{0:T(128)}, u32[]{:S(2)}) copy-start(f32[32]{0:T(128)} %param.21) | copy-start | bytes 388
  0.7 3.3 %copy-start.10 = (bf16[128,32]{0,1:T(8,128)(2,1)S(1)}, bf16[128,32]{0,1:T(8,128)(2,1)}, u32[]{:S(2)}) copy-start(bf16[128,32]{0,1:T(8,128)(2,1)} %param.20) | copy-start | bytes 24580
  0.7 3.3 %copy-start.2 = (bf16[256,1024]{1,0:T(8,128)(2,1)S(1)}, bf16[256,1024]{1,0:T(8,128)(2,1)}, u32[]{:S(2)}) copy-start(bf16[256,1024]{1,0:T(8,128)(2,1)} %attn_out_ref.1) | copy-start | bytes 1572868
  0.8 3.3 %copy-start.12 = (s32[128]{0:T(128)S(1)}, s32[128]{0:T(128)}, u32[]{:S(2)}) copy-start(s32[128]{0:T(128)} %param.17) | copy-start | bytes 1540
  0.8 3.3 %copy-start.11 = (s32[128]{0:T(128)S(1)}, s32[128]{0:T(128)}, u32[]{:S(2)}) copy-start(s32[128]{0:T(128)} %param.16) | copy-start | bytes 1540
  0.8 3.3 %copy-start.5 = (bf16[16,32,128]{2,1,0:T(8,128)(2,1)S(1)}, bf16[16,32,128]{2,1,0:T(8,128)(2,1)}, u32[]{:S(2)}) copy-start(bf16[16,32,128]{2,1,0:T(8,128)(2,1)} %param.15) | copy-start | bytes 393220

commit v3 on v2

--- a/solution.py
+++ b/solution.py
@@ -27,16 +27,16 @@
     nr,
     nc,
     head_width,
-    seq_ref,
-    pair_ref,
-    mask_ref,
-    chain_ref,
-    proj_ref,
-    attn_out_ref,
-    bias_w_ref,
-    chain_bias_ref,
-    outer_in_ref,
-    tri_in_ref,
+    seq_hbm,
+    pair_hbm,
+    mask_hbm,
+    chain_hbm,
+    attn_in_hbm,
+    attn_out_hbm,
+    bias_w_hbm,
+    chain_bias_hbm,
+    outer_in_hbm,
+    tri_in_hbm,
     outer_out_hbm,
     tri_out_hbm,
     up_hbm,
@@ -59,10 +59,21 @@
     right_all,
     prod_ref,
     prod_recv,
+    seq_ref,
+    pair_ref,
+    mask_ref,
+    chain_ref,
+    attn_in_ref,
+    attn_out_ref,
+    bias_w_ref,
+    chain_bias_ref,
+    outer_in_ref,
+    tri_in_ref,
     outer_out_ref,
     tri_out_ref,
     up_ref,
     down_ref,
+    proj_ref,
     row_send,
     row_recv,
     col_send,
@@ -73,7 +84,7 @@
 ):
     me_r = lax.axis_index("row")
     me_c = lax.axis_index("col")
-    rows, width = seq_ref.shape
+    rows, width = seq_hbm.shape
     pairs, chan = pair_ref.shape
     cols = pairs // rows
     length = mask_ref.shape[1]
@@ -89,20 +100,6 @@
     me_z = me_r // 2
     share = per_col // 2
 
-    loads = [
-        pltpu.make_async_copy(src, dst, load_sem.at[n])
-        for n, (src, dst) in enumerate(
-            (
-                (outer_out_hbm, outer_out_ref),
-                (tri_out_hbm, tri_out_ref),
-                (up_hbm, up_ref),
-                (down_hbm, down_ref),
-            )
-        )
-    ]
-    for load in loads:
-        load.start()
-
     def row_peer(d):
         return lax.rem(me_r + d, nr)
 
@@ -136,8 +133,56 @@
         pl.semaphore_signal(barrier, inc=1, device_id=(me_r, col_peer(d)), device_id_type=MESH)
         pl.semaphore_signal(barrier, inc=1, device_id=(partner, col_peer(d)), device_id_type=MESH)
 
+    loads = {}
+    for name, src, dst in (
+        ("seq", seq_hbm, seq_ref),
+        ("attn_in", attn_in_hbm, attn_in_ref),
+        ("pair", pair_hbm, pair_ref),
+        ("bias_w", bias_w_hbm, bias_w_ref),
+        ("mask", mask_hbm, mask_ref),
+        ("chain", chain_hbm, chain_ref),
+        ("chain_bias", chain_bias_hbm, chain_bias_ref),
+        ("attn_out", attn_out_hbm, attn_out_ref),
+        ("outer_in", outer_in_hbm, outer_in_ref),
+        ("outer_out", outer_out_hbm, outer_out_ref),
+        ("tri_in", tri_in_hbm, tri_in_ref),
+        ("tri_out", tri_out_hbm, tri_out_ref),
+        ("up", up_hbm, up_ref),
+        ("down", down_hbm, down_ref),
+    ):
+        loads[name] = pltpu.make_async_copy(src, dst, load_sem.at[len(loads)])
+        loads[name].start()
+
+    parts = attn_in_ref.shape[1]
+    loads["seq"].wait()
+    normed_seq = layer_norm(seq_ref[...].astype(F32)).astype(BF16)
+    lane_w = 128
+    pieces = width // lane_w
+    stacked = jnp.concatenate(
+        [normed_seq[:, n * lane_w : (n + 1) * lane_w] for n in range(pieces)], axis=0
+    )
+    spread_lane = lax.broadcasted_iota(jnp.int32, (lane_w, parts * lane_w), 1)
+    spread_sub = lax.broadcasted_iota(jnp.int32, (lane_w, parts * lane_w), 0)
+    spread = (spread_lane // parts == spread_sub).astype(F32).astype(BF16)
+    repeated = jnp.dot(stacked, spread, preferred_element_type=F32)
+    part_of = lax.broadcasted_iota(jnp.int32, (rows, parts * lane_w), 1) % parts
+    loads["attn_in"].wait()
+    projected = None
+    for n in range(pieces):
+        row_block = repeated[n * rows : (n + 1) * rows, :]
+        masked = jnp.concatenate(
+            [jnp.where(part_of == p, row_block, 0.0) for p in range(parts)], axis=0
+        ).astype(BF16)
+        weight = attn_in_ref[n * lane_w : (n + 1) * lane_w].reshape(parts * lane_w, feats)
+        term = jnp.dot(masked, weight, preferred_element_type=F32)
+        projected = term if projected is None else projected + term
+    for p in range(parts):
+        proj_ref[:, p * feats : (p + 1) * feats] = projected[p * rows : (p + 1) * rows, :]
+
     my_rows = pl.ds(pl.multiple_of(row_start, rows), rows)
     kv_all[my_rows, :] = proj_ref[:, feats : 3 * feats].astype(BF16)
+    loads["pair"].wait()
+    loads["bias_w"].wait()
     normed_pair = layer_norm(pair_ref[...].astype(F32)).astype(BF16)
     tile = nt_dot(bias_w_ref[...], normed_pair)
     for c in range(nc):
@@ -156,6 +201,8 @@
     lane_l = lax.broadcasted_iota(jnp.int32, (rows, length), 1)
     sub_l = lax.broadcasted_iota(jnp.int32, (rows, length), 0)
     mine = lane_l == sub_l + row_start
+    for name in ("mask", "chain", "chain_bias"):
+        loads[name].wait()
     chain_row = chain_ref[...]
     mask_row = mask_ref[...]
     chain_col = jnp.sum(
@@ -216,6 +263,7 @@
         axis=0,
     )
     mixed = (gate * gathered).astype(BF16)
+    loads["attn_out"].wait()
     upd[me_c] = jnp.dot(mixed, attn_out_ref[...], preferred_element_type=F32).astype(BF16)
     upd_copies = []
     for d in range(1, nc):
@@ -229,6 +277,7 @@
     sequence_out = (seq_ref[...].astype(F32) + update).astype(BF16)
     seq_out_ref[...] = sequence_out
     normed_out = layer_norm(sequence_out.astype(F32)).astype(BF16)
+    loads["outer_in"].wait()
     outer_rows = jnp.dot(normed_out, outer_in_ref[...], preferred_element_type=F32).astype(BF16)
     outer_all[my_rows, :] = outer_rows
     outer_copies = []
@@ -246,7 +295,8 @@
     live_k = jnp.sum(
         jnp.where(lane_c == sub_c + col_start, live_row, 0.0), axis=-1, keepdims=True
     )
-    loads[0].wait()
+    loads["outer_out"].wait()
+    loads["tri_in"].wait()
     for copy in outer_copies:
         copy.wait()
     right_rows = outer_all[pl.ds(pl.multiple_of(col_start, cols), cols), :].astype(F32)
@@ -376,8 +426,8 @@
         def _():
             prod_copy(0, d, slots[d]).wait_send()
 
-    for load in loads[1:]:
-        load.wait()
+    for name in ("tri_out", "up", "down"):
+        loads[name].wait()
     for i in range(rows):
         for b in range(per_col):
             total = prod_recv[0, b, i].astype(F32)
@@ -421,20 +471,16 @@
     heads_all = chain_bias.shape[0]
     heads = heads_all // nc
     head_width = feats // heads
-    normed_seq = layer_norm(sequence.astype(F32)).astype(BF16)
-    projected = jnp.einsum(
-        "id,dpe->ipe", normed_seq, attention_in, preferred_element_type=F32
-    ).reshape(rows, 4 * feats)
     pairs = rows * cols
     per_col = cols // rows
     vmem = pl.BlockSpec(memory_space=pltpu.VMEM)
     sequence_out, pair_out = pl.pallas_call(
         functools.partial(kernel, nr, nc, head_width),
         out_shape=(
-            jax.ShapeDtypeStruct((rows, width), BF16),
-            jax.ShapeDtypeStruct((pairs, chan), BF16),
+            pltpu.VMEM((rows, width), BF16),
+            pltpu.VMEM((pairs, chan), BF16),
         ),
-        in_specs=[vmem] * 10 + [pl.BlockSpec(memory_space=pltpu.HBM)] * 4,
+        in_specs=[pl.BlockSpec(memory_space=pltpu.HBM)] * 14,
         out_specs=(vmem, vmem),
         scratch_shapes=[
             pltpu.VMEM((nc, heads, pairs), F32),
@@ -453,27 +499,38 @@
             pltpu.VMEM((nr // 2, cols, rows, chan), BF16),
             pltpu.VMEM((2, nr // 2, rows, rows, chan), BF16),
             pltpu.VMEM((nc, per_col, rows, rows, chan), BF16),
+            pltpu.VMEM((rows, width), BF16),
+            pltpu.VMEM((pairs, chan), BF16),
+            pltpu.VMEM((1, length), jnp.int32),
+            pltpu.VMEM((1, length), jnp.int32),
+            pltpu.VMEM(attention_in.shape, BF16),
+            pltpu.VMEM(attention_out.shape, BF16),
+            pltpu.VMEM((heads_all, chan), BF16),
+            pltpu.VMEM((1, heads_all), F32),
+            pltpu.VMEM(outer_in.shape, BF16),
+            pltpu.VMEM((triangle_in.shape[1], chan, chan), BF16),
             pltpu.VMEM(outer_out.shape, BF16),
             pltpu.VMEM(triangle_out.shape, BF16),
             pltpu.VMEM(transition_up.shape, BF16),
             pltpu.VMEM(transition_down.shape, BF16),
+            pltpu.VMEM((rows, 4 * feats), F32),
             pltpu.SemaphoreType.DMA((3, nr)),
             pltpu.SemaphoreType.DMA((3, nr)),
             pltpu.SemaphoreType.DMA((2, nc)),
             pltpu.SemaphoreType.DMA((2, nc)),
             pltpu.SemaphoreType.DMA((2, nr // 2)),
             pltpu.SemaphoreType.DMA((2, nc * (per_col // 2))),
-            pltpu.SemaphoreType.DMA((4,)),
+            pltpu.SemaphoreType.DMA((14,)),
         ],
         compiler_params=pltpu.CompilerParams(
-            collective_id=0, has_side_effects=True, vmem_limit_bytes=48 * 1024 * 1024
+            collective_id=0, has_side_effects=True, vmem_limit_bytes=56 * 1024 * 1024
         ),
     )(
         sequence,
         pair_state.reshape(pairs, chan),
         residue_mask.reshape(1, length),
         chain_index.reshape(1, length),
-        projected,
+        attention_in,
         attention_out,
         bias_weight.T,
         chain_bias.reshape(1, heads_all),

time: 44.5 us -> 40.8 us (0.917)
  other arithmetic: 1.99 us -> 0 us
  matrix products: 1.18 us -> 0 us
    reduce_sum x2 -> x0, other arithmetic: 1.98 us -> none  [the longest x1 1.03 us: layer_norm(): center = values - jnp.mean(values, axis=-1, keepdims=True)]
    dot_general x1 -> x0, matrix products: 1.18 us -> none  [per_device(): jnp.einsum('id,dpe->ipe', normed_seq, attention_in, preferred_element_typ...]
    unnamed x30 -> x2, local copies, waits for them, and re-layouts: 1.34 us -> 1.27 us
where the time goes in v3:
time: 40.8 us; the launch traced here: 40.7 us
  Pallas kernels  38.8 us (95%)
  local copies, waits for them, and re-layouts  1.27 us (3%)
  between operations  0.64 us (2%)
    pallas_call x1, Pallas kernels, per_device(): pl.pallas_call(functools.partial(kernel, nr, nc, head_width), out_shape=(...  38.8 us
    unnamed x2, local copies, waits for them, and re-layouts  1.27 us

profile of v3, /device:TPU:24, one launch (start us, length us, event | category | flops | bytes accessed | tf_op | source)
XLA Modules:
  0.0 40.7 jit_solution(11061523604866081722)
XLA Ops:
  0.6 38.8 %shard_map.149 = (bf16[16,1024]{1,0:T(8,128)(2,1)S(1)}, bf16[512,128]{1,0:T(8,128)(2,1)S(1)}) custom-call(bf16[16,1024]{1,0:T(8,128)(2,1)} %seq_hbm.1, bf16[512,128]{1,0:T(8,128)(2,1)} %bitcast.9, s32[1,128]{1,0:T(1,128)} %bitcast.11, s32[1,128]{1,0:T(1,128)} %bitcast.12, bf16[1024,4,256]{2,1,0:T(4,128)(2,1)} %attn_in_hbm.1, bf16[256,1024]{1,0:T(8,128)(2,1)} %attn_out_hbm.1, ...), custom_call_target="tpu_custom_call" | custom-call | tf_op jit(solution)/shard_map/pallas_call | solution.py:477
  39.4 0.6 %copy.18 = bf16[16,1024]{1,0:T(8,128)(2,1)} copy(bf16[16,1024]{1,0:T(8,128)(2,1)S(1)} %get-tuple-element.6) | data formatting | bytes 65536
  40.0 0.7 %copy.19 = bf16[16,32,128]{2,1,0:T(8,128)(2,1)} copy(bf16[16,32,128]{2,1,0:T(8,128)(2,1)S(1)} %bitcast.7) | data formatting | bytes 262144
